TPU v7x, 32 devices: a whole 2x2x4 slice. The times are simulated.
32 devices in a mesh: dp: 8 (over z, x), tensor: 4 (over y, core).
Axes of the slice: x: 2, y: 2, z: 4, core: 2. Of those that a mesh axis runs over, the one named last changes fastest.
Arguments:
- layer_input: bfloat16 [12288, 768], P('dp'), may hold values from -6 to 6
- patch_coords: int32 [3, 12288], P(None, 'dp'), may hold values from 0 to 55, as said below
- item_lengths: int32 [32], P('dp'), may hold values from 0 to 1536, as said below
- out_grad: bfloat16 [12288, 768], P('dp'), may hold values from -6 to 6
- ln1_gain: bfloat16 [768], replicated, may hold values from 0.25 to 1.75
- ln1_shift: bfloat16 [768], replicated, may hold values from -1.75 to 1.75
- w_qkv: bfloat16 [768, 3, 768], P(None, None, 'tensor'), may hold values from -0.21875 to 0.21875
- b_qv: bfloat16 [2, 768], P(None, 'tensor'), may hold values from -3 to 3
- w_out: bfloat16 [768, 768], P('tensor'), may hold values from -0.875 to 0.875
- b_out: bfloat16 [768], replicated, may hold values from -1.75 to 1.75
- ln2_gain: bfloat16 [768], replicated, may hold values from 0.25 to 1.75
- ln2_shift: bfloat16 [768], replicated, may hold values from -1.75 to 1.75
- w_fc1: bfloat16 [768, 3072], P(None, 'tensor'), may hold values from -0.21875 to 0.21875
- b_fc1: bfloat16 [3072], P('tensor'), may hold values from -3 to 3
- w_fc2: bfloat16 [3072, 768], P('tensor'), may hold values from -0.109375 to 0.109375
- b_fc2: bfloat16 [768], replicated, may hold values from -1.75 to 1.75
Outputs:
- layer_output: bfloat16 [12288, 768], P('dp')
- input_grad: float32 [12288, 768], P('dp')
- grad_ln1_gain: float32 [768], replicated
- grad_ln1_shift: float32 [768], replicated
- grad_w_qkv: float32 [768, 3, 768], P(None, None, 'tensor')
- grad_b_qv: float32 [2, 768], P(None, 'tensor')
- grad_w_out: float32 [768, 768], P('tensor')
- grad_b_out: float32 [768], replicated
- grad_ln2_gain: float32 [768], replicated
- grad_ln2_shift: float32 [768], replicated
- grad_w_fc1: float32 [768, 3072], P(None, 'tensor')
- grad_b_fc1: float32 [3072], P('tensor')
- grad_w_fc2: float32 [3072, 768], P('tensor')
- grad_b_fc2: float32 [768], replicated
Inputs may be any that keep to these rules, and one draw needn't show every extreme that they name: `item_lengths`: A row of 8 takes 4 consecutive entries: its items' visible lengths, laid out one after another from the row's first slot, summing to at most 1536; the remaining slots are padding. In every draw some row holds a single item of 1536 tokens. `patch_coords`: row 0 is the token's frame, 0 to 2; rows 1 and 2 are its patch row and column.
All inputs are finite; a program needn't handle non-finite values.
Results may differ from a plain program's by a relative error of at most 0.018.
Values may be sent and summed in bfloat16 or wider, within the bound.
A program may use at most 128 MiB of HBM per device.

v0:
```python
from functools import partial
import math
import jax
import jax.numpy as jnp
from jax import lax
from jax.sharding import PartitionSpec as P

HEAD_DIM = 64
NORM_EPS = 1e-06
MASK_FILL = -1e30


def layer_norm(values_in, norm_gain, norm_shift):
    mean_row = jnp.mean(values_in, axis=-1, keepdims=True)
    centred = values_in - mean_row
    spread = jnp.mean(centred * centred, axis=-1, keepdims=True)
    return centred * lax.rsqrt(spread + NORM_EPS) * norm_gain + norm_shift


def sincos_table(coords, feature_count):
    half_width = feature_count // 6
    ladder = jnp.arange(half_width, dtype=jnp.float32) / half_width
    frequency = jnp.power(10000.0, -ladder)
    angles = coords.astype(jnp.float32)[:, :, None] * frequency[None, None, :]
    wave_parts = jnp.concatenate([jnp.sin(angles), jnp.cos(angles)], axis=2)
    return jnp.concatenate([wave_parts[0], wave_parts[1], wave_parts[2]], axis=1)


def item_layout(length_rows, token_count, slot_count):
    item_ends = jnp.cumsum(length_rows, axis=1, dtype=jnp.int32)
    places = jnp.arange(token_count, dtype=jnp.int32)
    passed = (places[None, :, None] >= item_ends[:, None, :]).astype(jnp.int32)
    item_of = jnp.sum(passed, axis=2, dtype=jnp.int32)
    visible = places[None, :] < item_ends[:, -1:]
    return (jnp.where(visible, item_of, slot_count + places[None, :]), visible)


def block_scores(query_block, key_rows, segment_block, segment):
    score_scale = 1.0 / math.sqrt(key_rows.shape[2])
    scores = (
        jnp.einsum("qhd,khd->hqk", query_block, key_rows, preferred_element_type=jnp.float32)
        * score_scale
    )
    allowed = (segment_block[:, None] == segment[None, :])[None]
    return jnp.where(allowed, scores, MASK_FILL)


def attend_forward(query_rows, key_rows, value_rows, segment):
    row_count = query_rows.shape[0]
    block_rows = min(512, row_count)

    def attend_block(block_index):
        block_start = block_index * block_rows
        query_block = lax.dynamic_slice_in_dim(query_rows, block_start, block_rows, 0)
        segment_block = lax.dynamic_slice_in_dim(segment, block_start, block_rows, 0)
        scores = block_scores(query_block, key_rows, segment_block, segment)
        row_max = jnp.max(scores, axis=2, keepdims=True)
        raised = jnp.exp(scores - row_max)
        row_total = jnp.sum(raised, axis=2, keepdims=True)
        weights = (raised / row_total).astype(jnp.bfloat16)
        mixed = jnp.einsum("hqk,khd->qhd", weights, value_rows, preferred_element_type=jnp.float32)
        return (mixed, (row_max + jnp.log(row_total))[:, :, 0])

    mixed_all, log_totals = lax.map(attend_block, jnp.arange(row_count // block_rows))
    return (mixed_all.reshape(query_rows.shape), log_totals)


def attend_backward(query_rows, key_rows, value_rows, segment, mixed_grad, log_totals):
    row_count = query_rows.shape[0]
    block_rows = min(512, row_count)
    score_scale = 1.0 / math.sqrt(key_rows.shape[2])
    zeros_kv = jnp.zeros(key_rows.shape, jnp.float32)

    def back_block(running, inputs):
        block_index, lse_block = inputs
        key_acc, value_acc = running
        block_start = block_index * block_rows
        query_block = lax.dynamic_slice_in_dim(query_rows, block_start, block_rows, 0)
        segment_block = lax.dynamic_slice_in_dim(segment, block_start, block_rows, 0)
        grad_block = lax.dynamic_slice_in_dim(mixed_grad, block_start, block_rows, 0)
        scores = block_scores(query_block, key_rows, segment_block, segment)
        weights = jnp.exp(scores - lse_block[:, :, None])
        weight_grad = jnp.einsum(
            "qhd,khd->hqk", grad_block, value_rows, preferred_element_type=jnp.float32
        )
        centre = jnp.sum(weights * weight_grad, axis=2, keepdims=True)
        score_grad = (weights * (weight_grad - centre)).astype(jnp.bfloat16)
        query_grad = (
            jnp.einsum("hqk,khd->qhd", score_grad, key_rows, preferred_element_type=jnp.float32)
            * score_scale
        )
        key_acc = (
            key_acc
            + jnp.einsum(
                "hqk,qhd->khd", score_grad, query_block, preferred_element_type=jnp.float32
            )
            * score_scale
        )
        value_acc = value_acc + jnp.einsum(
            "hqk,qhd->khd",
            weights.astype(jnp.bfloat16),
            grad_block,
            preferred_element_type=jnp.float32,
        )
        return ((key_acc, value_acc), query_grad)

    block_list = jnp.arange(row_count // block_rows)
    (key_grad, value_grad), query_grad = lax.scan(
        back_block, (zeros_kv, zeros_kv), (block_list, log_totals)
    )
    return (query_grad.reshape(query_rows.shape), key_grad, value_grad)


def run_forward(hidden_in, segment, visible, params, second_pass):
    (
        ln1_gain,
        ln1_shift,
        w_qkv,
        b_qv,
        w_out,
        b_out,
        ln2_gain,
        ln2_shift,
        w_fc1,
        b_fc1,
        w_fc2,
        b_fc2,
    ) = params
    row_count = hidden_in.shape[0]
    heads_here = w_out.shape[0] // HEAD_DIM
    head_shape = (row_count, heads_here, HEAD_DIM)
    normed_one = layer_norm(
        hidden_in, ln1_gain.astype(jnp.float32), ln1_shift.astype(jnp.float32)
    ).astype(jnp.bfloat16)
    projected = jnp.einsum("td,dcj->tcj", normed_one, w_qkv, preferred_element_type=jnp.float32)
    query_rows = (
        (projected[:, 0] + b_qv[0].astype(jnp.float32)).astype(jnp.bfloat16).reshape(head_shape)
    )
    key_rows = projected[:, 1].astype(jnp.bfloat16).reshape(head_shape)
    value_rows = (
        (projected[:, 2] + b_qv[1].astype(jnp.float32)).astype(jnp.bfloat16).reshape(head_shape)
    )
    mixed, log_totals = attend_forward(query_rows, key_rows, value_rows, segment)
    mixed_low = mixed.reshape(row_count, -1).astype(jnp.bfloat16)
    attn_part = jnp.dot(mixed_low, w_out, preferred_element_type=jnp.float32).astype(jnp.bfloat16)
    if second_pass:
        attn_total = lax.psum(attn_part, "tensor").astype(jnp.float32)
    else:
        attn_total = lax.psum(attn_part, "tensor").astype(jnp.float32)
    middle = hidden_in + attn_total + b_out.astype(jnp.float32)
    normed_two = layer_norm(
        middle, ln2_gain.astype(jnp.float32), ln2_shift.astype(jnp.float32)
    ).astype(jnp.bfloat16)
    hidden_pre = jnp.dot(normed_two, w_fc1, preferred_element_type=jnp.float32) + b_fc1.astype(
        jnp.float32
    )
    activated = jax.nn.gelu(hidden_pre, approximate=False).astype(jnp.bfloat16)
    kept_state = (
        normed_one,
        query_rows,
        key_rows,
        value_rows,
        log_totals,
        mixed_low,
        middle,
        normed_two,
        hidden_pre,
        activated,
    )
    if second_pass:
        return (None, kept_state)
    mlp_part = jnp.dot(activated, w_fc2, preferred_element_type=jnp.float32).astype(jnp.bfloat16)
    mlp_total = lax.psum(mlp_part, "tensor").astype(jnp.float32)
    result = jnp.where(visible[:, None], middle + mlp_total + b_fc2.astype(jnp.float32), 0.0)
    return (result, kept_state)


def sum_gradients(grads):
    large = [g.ndim == 2 and g.shape[0] > 2 or g.ndim == 3 for g in grads]
    low = lax.psum([g.astype(jnp.bfloat16) for g, w in zip(grads, large) if w], "dp")
    wide = lax.psum([g for g, w in zip(grads, large) if not w], "dp")
    return [low.pop(0).astype(jnp.float32) if w else wide.pop(0) for w in large]


def on_device(
    layer_input,
    patch_coords,
    item_lengths,
    out_grad,
    ln1_gain,
    ln1_shift,
    w_qkv,
    b_qv,
    w_out,
    b_out,
    ln2_gain,
    ln2_shift,
    w_fc1,
    b_fc1,
    w_fc2,
    b_fc2,
):
    segment_rows, visible_rows = item_layout(
        item_lengths.reshape(1, -1), layer_input.shape[0], item_lengths.shape[0]
    )
    segment = segment_rows[0]
    visible = visible_rows[0]
    hidden_in = layer_input.astype(jnp.float32) + sincos_table(patch_coords, layer_input.shape[1])
    params = (
        ln1_gain,
        ln1_shift,
        w_qkv,
        b_qv,
        w_out,
        b_out,
        ln2_gain,
        ln2_shift,
        w_fc1,
        b_fc1,
        w_fc2,
        b_fc2,
    )
    result, kept_state = run_forward(hidden_in, segment, visible, params, False)
    (
        normed_one,
        query_rows,
        key_rows,
        value_rows,
        log_totals,
        mixed_low,
        middle,
        normed_two,
        hidden_pre,
        activated,
    ) = kept_state
    top_grad = jnp.where(visible[:, None], out_grad, jnp.zeros_like(out_grad))
    top_grad_wide = top_grad.astype(jnp.float32)
    grad_b_fc2 = jnp.sum(top_grad_wide, axis=0)
    grad_w_fc2 = jnp.einsum("tf,td->fd", activated, top_grad, preferred_element_type=jnp.float32)
    act_grad = jnp.einsum("td,fd->tf", top_grad, w_fc2, preferred_element_type=jnp.float32)
    gelu_value, gelu_back = jax.vjp(partial(jax.nn.gelu, approximate=False), hidden_pre)
    pre_grad = gelu_back(act_grad)[0].astype(jnp.bfloat16)
    grad_b_fc1 = jnp.sum(pre_grad.astype(jnp.float32), axis=0)
    grad_w_fc1 = jnp.einsum("td,tf->df", normed_two, pre_grad, preferred_element_type=jnp.float32)
    norm_grad_part = jnp.einsum("tf,df->td", pre_grad, w_fc1, preferred_element_type=jnp.float32)
    norm_grad_two = lax.psum(norm_grad_part.astype(jnp.bfloat16), "tensor").astype(jnp.float32)
    unused_two, norm_back_two = jax.vjp(
        layer_norm, middle, ln2_gain.astype(jnp.float32), ln2_shift.astype(jnp.float32)
    )
    middle_ln, grad_ln2_gain, grad_ln2_shift = norm_back_two(norm_grad_two)
    middle_grad = top_grad_wide + middle_ln
    grad_b_out = jnp.sum(middle_grad, axis=0)
    middle_low = middle_grad.astype(jnp.bfloat16)
    grad_w_out = jnp.einsum("tj,td->jd", mixed_low, middle_low, preferred_element_type=jnp.float32)
    mixed_grad = (
        jnp.einsum("td,jd->tj", middle_low, w_out, preferred_element_type=jnp.float32)
        .astype(jnp.bfloat16)
        .reshape(query_rows.shape)
    )
    query_grad, key_grad, value_grad = attend_backward(
        query_rows, key_rows, value_rows, segment, mixed_grad, log_totals
    )
    row_count = query_rows.shape[0]
    proj_grad = (
        jnp.stack([query_grad, key_grad, value_grad], axis=1)
        .astype(jnp.bfloat16)
        .reshape(row_count, 3, -1)
    )
    grad_b_qv = jnp.sum(proj_grad[:, 0::2].astype(jnp.float32), axis=0)
    grad_w_qkv = jnp.einsum(
        "td,tcj->dcj", normed_one, proj_grad, preferred_element_type=jnp.float32
    )
    norm_grad_first = jnp.einsum(
        "tcj,dcj->td", proj_grad, w_qkv, preferred_element_type=jnp.float32
    )
    norm_grad_one = lax.psum(norm_grad_first.astype(jnp.bfloat16), "tensor").astype(jnp.float32)
    unused_one, norm_back_one = jax.vjp(
        layer_norm, hidden_in, ln1_gain.astype(jnp.float32), ln1_shift.astype(jnp.float32)
    )
    input_ln, grad_ln1_gain, grad_ln1_shift = norm_back_one(norm_grad_one)
    input_grad = middle_grad + input_ln
    (
        grad_ln1_gain,
        grad_ln1_shift,
        grad_w_qkv,
        grad_b_qv,
        grad_w_out,
        grad_b_out,
        grad_ln2_gain,
        grad_ln2_shift,
        grad_w_fc1,
        grad_b_fc1,
        grad_w_fc2,
        grad_b_fc2,
    ) = sum_gradients(
        (
            grad_ln1_gain,
            grad_ln1_shift,
            grad_w_qkv,
            grad_b_qv,
            grad_w_out,
            grad_b_out,
            grad_ln2_gain,
            grad_ln2_shift,
            grad_w_fc1,
            grad_b_fc1,
            grad_w_fc2,
            grad_b_fc2,
        )
    )
    return (
        result.astype(jnp.bfloat16),
        input_grad,
        grad_ln1_gain,
        grad_ln1_shift,
        grad_w_qkv,
        grad_b_qv,
        grad_w_out,
        grad_b_out,
        grad_ln2_gain,
        grad_ln2_shift,
        grad_w_fc1,
        grad_b_fc1,
        grad_w_fc2,
        grad_b_fc2,
    )


def solution(mesh):
    placed = (
        P("dp", None),
        P(None, "dp"),
        P("dp"),
        P("dp", None),
        P(),
        P(),
        P(None, None, "tensor"),
        P(None, "tensor"),
        P("tensor", None),
        P(),
        P(),
        P(),
        P(None, "tensor"),
        P("tensor"),
        P("tensor", None),
        P(),
    )
    return jax.shard_map(
        on_device,
        mesh=mesh,
        in_specs=placed,
        out_specs=(
            P("dp", None),
            P("dp", None),
            P(),
            P(),
            P(None, None, "tensor"),
            P(None, "tensor"),
            P("tensor", None),
            P(),
            P(),
            P(),
            P(None, "tensor"),
            P("tensor"),
            P("tensor", None),
            P(),
        ),
        check_vma=False,
    )
```

profile of v0, /device:TPU:0, one launch (start us, length us, event | category | flops | bytes accessed | tf_op | source)
XLA Modules:
  0.0 612.9 jit_solution(17201050054439104026)
XLA Ops:
  8.1 8.3 %multiply_sine_fusion = (f32[3,1536,128]{2,1,0:T(8,128)S(1)}, f32[3,1536,128]{2,1,0:T(8,128)S(1)}) fusion(f32[128]{0:T(128)S(1)} %negate_power_fusion, f32[3,1536]{1,0:T(4,128)S(1)} %convert_element_type.153), kind=kLoop, calls=%fused_computation.89 | loop fusion | flops 589824 | bytes 4737536 | tf_op jit(solution)/shard_map/sin | solution.py:25
  29.3 39.0 %while.27 = (s32[]{:T(128)}, bf16[3,512,3,64]{1,3,2,0:T(8,128)(2,1)S(1)}, f32[3,3,512]{2,1,0:T(4,128)}, s32[3]{0:T(128)S(1)}, s32[1536]{0:T(1024)}, /*index=5*/s...) while((s32[]{:T(128)}, ...), condition=%wide.region_7.8_spmd, body=%wide.region_4.7_spmd.sunk | while | flops 633076224 | bytes 33307488 | solution.py:64
  77.6 53.4 %all-reduce.8.cloned.1.call-done = bf16[1536,768]{1,0:T(8,128)(2,1)} async-done(((bf16[1536,768]{1,0:T(8,128)(2,1)}), bf16[1536,768]{1,0:T(8,128)(2,1)}) %all-reduce.8.cloned.1.call-update) | async-done | bytes 2359312 | tf_op jit(solution)/shard_map/psum | solution.py:149
  137.1 12.8 %multiply_convert_fusion.1 = (bf16[1536,768]{1,0:T(8,128)(2,1)}, f32[1536,768]{1,0:T(8,128)S(1)}, f32[1536,768]{1,0:T(8,128)S(1)}) fusion(f32[768]{0:T(1024)S(1)} %copy-done.49, bf16[1536,768]{1,0:T(8,128)(2,1)S(1)} %add_convert_fusion.1, bf16[768,768]{1,0:T(8,128)(2,1)S(1)} %copy-done), kind=kOutput, calls=%fused_computation.69 | convolution fusion | flops 1889796096 | bytes 15338496 | tf_op jit(solution)/shard_map/dot_general | solution.py:154
  149.9 4.6 convert_reduce_fusion.3
  159.4 5.4 convolution_convert_fusion.1
  164.8 50.4 %all-reduce.10.cloned.1.call-done = bf16[1536,768]{1,0:T(8,128)(2,1)} async-done(((bf16[1536,768]{1,0:T(8,128)(2,1)}), bf16[1536,768]{1,0:T(8,128)(2,1)}) %all-reduce.10.cloned.1.call-update) | async-done | bytes 2359312 | tf_op jit(solution)/shard_map/psum | solution.py:246
  215.2 5.3 convert_reduce_fusion.1
  220.6 5.2 fusion.38
  225.8 5.2 fusion.57
  235.9 114.1 %while.28 = (s32[]{:T(128)}, f32[1536,3,64]{0,2,1:T(8,128)}, f32[1536,3,64]{0,2,1:T(8,128)S(1)}, bf16[3,512,3,64]{1,3,2,0:T(8,128)(2,1)}, s32[3]{0:T(128)S(1)}, ...) while((s32[]{:T(128)}, f32[1536,3,64]{0,2,1:T(8,128)}, ...), condition=%wide.region_17.18_spmd.clone, body=%wide.region_15.17_spmd.clone.sunk | while | flops 1533540864 | bytes 113105432 | solution.py:108
  237.1 6.0 fusion.122
  245.1 8.1 %multiply_reduce_fusion.4 = (f32[3,512]{1,0:T(4,128)S(1)}, f32[3,512,1536]{2,1,0:T(8,128)}) fusion(f32[3,512,1536]{2,1,0:T(8,128)} %fusion.122, f32[3,512]{1,0:T(4,128)S(1)} %dynamic-slice_bitcast_fusion.2, bf16[1536,3,64]{0,2,1:T(8,128)(2,1)S(1)} %get-tuple-element.476, bf16[1536,3,64]{0,2,1:T(8,128)(2,1)} %get-tuple-element.473, ...), kind=kOutput, calls=%fused_computation.16.clone.1 | convolution fusion | flops 313784832 | bytes 20459524 | tf_op jit(solution)/shard_map/while/body/eval_jaxpr/qhd,khd->hqk/dot_general | solution.py:41
  253.3 9.4 %multiply_convert_fusion.3 = bf16[3,512,1536]{2,1,0:T(8,128)(2,1)} fusion(f32[3,512,1536]{2,1,0:T(8,128)} %get-tuple-element.395, f32[3,512,1536]{2,1,0:T(8,128)} %fusion.122, f32[3,512]{1,0:T(4,128)S(1)} %get-tuple-element.396), kind=kLoop, calls=%fused_computation.15.clone.1 | loop fusion | flops 7077888 | bytes 23599104 | tf_op jit(solution)/shard_map/while/body/eval_jaxpr/convert_element_type | solution.py:87
  269.1 4.9 fusion.124
  275.2 6.0 fusion.122
  283.2 8.1 %multiply_reduce_fusion.4 = (f32[3,512]{1,0:T(4,128)S(1)}, f32[3,512,1536]{2,1,0:T(8,128)}) fusion(f32[3,512,1536]{2,1,0:T(8,128)} %fusion.122, f32[3,512]{1,0:T(4,128)S(1)} %dynamic-slice_bitcast_fusion.2, bf16[1536,3,64]{0,2,1:T(8,128)(2,1)S(1)} %get-tuple-element.476, bf16[1536,3,64]{0,2,1:T(8,128)(2,1)} %get-tuple-element.473, ...), kind=kOutput, calls=%fused_computation.16.clone.1 | convolution fusion | flops 313784832 | bytes 20459524 | tf_op jit(solution)/shard_map/while/body/eval_jaxpr/qhd,khd->hqk/dot_general | solution.py:41
  291.3 9.4 %multiply_convert_fusion.3 = bf16[3,512,1536]{2,1,0:T(8,128)(2,1)} fusion(f32[3,512,1536]{2,1,0:T(8,128)} %get-tuple-element.395, f32[3,512,1536]{2,1,0:T(8,128)} %fusion.122, f32[3,512]{1,0:T(4,128)S(1)} %get-tuple-element.396), kind=kLoop, calls=%fused_computation.15.clone.1 | loop fusion | flops 7077888 | bytes 23599104 | tf_op jit(solution)/shard_map/while/body/eval_jaxpr/convert_element_type | solution.py:87
  307.1 4.9 fusion.124
  313.2 6.0 fusion.122
  321.2 8.1 %multiply_reduce_fusion.4 = (f32[3,512]{1,0:T(4,128)S(1)}, f32[3,512,1536]{2,1,0:T(8,128)}) fusion(f32[3,512,1536]{2,1,0:T(8,128)} %fusion.122, f32[3,512]{1,0:T(4,128)S(1)} %dynamic-slice_bitcast_fusion.2, bf16[1536,3,64]{0,2,1:T(8,128)(2,1)S(1)} %get-tuple-element.476, bf16[1536,3,64]{0,2,1:T(8,128)(2,1)} %get-tuple-element.473, ...), kind=kOutput, calls=%fused_computation.16.clone.1 | convolution fusion | flops 313784832 | bytes 20459524 | tf_op jit(solution)/shard_map/while/body/eval_jaxpr/qhd,khd->hqk/dot_general | solution.py:41
  329.4 9.4 %multiply_convert_fusion.3 = bf16[3,512,1536]{2,1,0:T(8,128)(2,1)} fusion(f32[3,512,1536]{2,1,0:T(8,128)} %get-tuple-element.395, f32[3,512,1536]{2,1,0:T(8,128)} %fusion.122, f32[3,512]{1,0:T(4,128)S(1)} %get-tuple-element.396), kind=kLoop, calls=%fused_computation.15.clone.1 | loop fusion | flops 7077888 | bytes 23599104 | tf_op jit(solution)/shard_map/while/body/eval_jaxpr/convert_element_type | solution.py:87
  345.2 4.9 fusion.124
  354.2 4.6 bitcast_convert_fusion
  358.9 5.6 convolution_convert_fusion.5
  372.3 80.8 %all-reduce.14.cloned.1.call-done = (bf16[1536,768]{1,0:T(8,128)(2,1)}, bf16[1536,768]{1,0:T(8,128)(2,1)}) async-done(((bf16[1536,768]{1,0:T(8,128)(2,1)}, bf16[1536,768]{1,0:T(8,128)(2,1)}), (bf16[1536,768]{1,0:T(8,128)(2,1)}, bf16[1536,768]{1,0:T(8,128)(2,1)})) %all-reduce.14.cloned.1.call-update) | async-done | bytes 4718608 | tf_op jit(solution)/shard_map/psum | solution.py:173
  453.1 4.7 convert_reduce_fusion
  457.9 4.3 fusion.39
  462.3 40.5 %all-reduce = (f32[768]{0:T(1024)}, f32[768]{0:T(1024)}, f32[2,192]{1,0:T(2,128)}, f32[768]{0:T(1024)}, f32[768]{0:T(1024)}, /*index=5*/f32[768]{0:T(1024)}, f32[768]{0:T(1024)}, f32[768]{0:T(1024)}) all-reduce(f32[768]{0:T(1024)S(1)} %get-tuple-element.172, ...), channel_id=1, replica_groups=mesh['dp'=8,'tensor'=4] {'dp'}, use_global_device_ids=true, to_apply=%region_22.23 | all-reduce | flops 5760 | bytes 46080 | tf_op jit(solution)/shard_map/psum | solution.py:181
  502.9 4.8 select_convert_fusion
  508.8 4.8 add_add_fusion.2
  513.6 84.2 %all-reduce.12.cloned.1.call-done = (bf16[768,3,192]{0,2,1:T(8,128)(2,1)}, bf16[192,768]{1,0:T(8,128)(2,1)}, bf16[768,768]{1,0:T(8,128)(2,1)}, bf16[768,768]{1,0:T(8,128)(2,1)}) async-done(((bf16[768,3,192]{0,2,1:T(8,128)(2,1)}, bf16[192,768]{1,0:T(8,128)(2,1)}, bf16[768,768]{1,0:T(8,128)(2,1)}, bf16[768,768]{1,0:T(8,128)(2,1)}), (bf16[768,3,192]{0,2,1:T(8,128)(2,1)}, bf16[192,768]{1,0:T(8,128)(2,1)}, ...) | async-done | bytes 3538960 | tf_op jit(solution)/shard_map/psum | solution.py:180
  (290 shorter events, 122.7 us)
Async XLA Ops:
  7.2 129.8 %copy-start = (bf16[768,768]{1,0:T(8,128)(2,1)S(1)}, bf16[768,768]{1,0:T(8,128)(2,1)}, u32[]{:S(2)}) copy-start(bf16[768,768]{1,0:T(8,128)(2,1)} %param.32) | copy-start | bytes 3538948
  7.2 123.8 %all-reduce.8.cloned.1.call-start = ((), (), s32[]{:S(2)}) async-start(), calls=%async_computation | async-start | bytes 4718592 | tf_op jit(solution)/shard_map/psum | solution.py:149
  68.3 66.5 %copy-start.8 = (bf16[1536,3,64]{0,2,1:T(8,128)(2,1)}, bf16[1536,3,64]{0,2,1:T(8,128)(2,1)S(1)}, u32[]{:S(2)}) copy-start(bf16[1536,3,64]{0,2,1:T(8,128)(2,1)S(1)} %get-tuple-element.500) | copy-start | bytes 1769476
  69.0 65.8 %copy-start.12 = (bf16[24,8,3,512]{3,1,2,0:T(8,128)(2,1)}, bf16[24,8,3,512]{3,1,2,0:T(8,128)(2,1)S(1)}, u32[]{:S(2)}) copy-start(bf16[24,8,3,512]{3,1,2,0:T(8,128)(2,1)S(1)} %copy.35) | copy-start | bytes 1769476
  72.5 142.8 %all-reduce.10.cloned.1.call-start = ((), (), s32[]{:S(2)}) async-start(), calls=%async_computation.1 | async-start | bytes 4718592 | tf_op jit(solution)/shard_map/psum | solution.py:246
  135.5 14.3 %copy-start.38 = (f32[1536]{0:T(1024)}, f32[1536]{0:T(1024)S(1)}, u32[]{:S(2)}) copy-start(f32[1536]{0:T(1024)S(1)} %multiply_reduce_fusion.1) | copy-start | bytes 18436
  135.6 14.3 %copy-start.30 = (f32[1536]{0:T(1024)}, f32[1536]{0:T(1024)S(1)}, u32[]{:S(2)}) copy-start(f32[1536]{0:T(1024)S(1)} %fusion.53) | copy-start | bytes 18436
  137.0 12.8 %copy-start.22 = (bf16[1536,768]{1,0:T(8,128)(2,1)}, bf16[1536,768]{1,0:T(8,128)(2,1)S(1)}, u32[]{:S(2)}) copy-start(bf16[1536,768]{1,0:T(8,128)(2,1)S(1)} %add_convert_fusion.1) | copy-start | bytes 7077892
  137.0 12.8 %copy-start.17 = (bf16[1536,768]{1,0:T(8,128)(2,1)S(1)}, bf16[1536,768]{1,0:T(8,128)(2,1)}, u32[]{:S(2)}) copy-start(bf16[1536,768]{1,0:T(8,128)(2,1)} %param.23) | copy-start | bytes 7077892
  137.0 12.8 %copy-start.40 = (pred[1536]{0:T(1024)(128)(4,1)S(1)}, pred[1536]{0:T(1024)(128)(4,1)}, u32[]{:S(2)}) copy-start(pred[1536]{0:T(1024)(128)(4,1)} %iota_compare_fusion.1) | copy-start | bytes 4612
  137.1 12.8 %copy-start.55 = (bf16[768,768]{1,0:T(8,128)(2,1)S(1)}, bf16[768,768]{1,0:T(8,128)(2,1)}, u32[]{:S(2)}) copy-start(bf16[768,768]{1,0:T(8,128)(2,1)} %param.34) | copy-start | bytes 3538948
  159.4 293.7 %all-reduce.14.cloned.1.call-start = ((), (), s32[]{:S(2)}) async-start(), calls=%async_computation.3 | async-start | bytes 9437184 | tf_op jit(solution)/shard_map/psum | solution.py:173
  159.4 55.8 %copy-start.35 = (f32[768]{0:T(1024)S(1)}, f32[768]{0:T(1024)}, u32[]{:S(2)}) copy-start(f32[768]{0:T(1024)} %convert_element_type.166) | copy-start | bytes 9220
  164.8 55.8 %copy-start.39 = (f32[1536]{0:T(1024)S(1)}, f32[1536]{0:T(1024)}, u32[]{:S(2)}) copy-start(f32[1536]{0:T(1024)} %copy-done.38) | copy-start | bytes 18436
  164.8 55.8 %copy-start.31 = (f32[1536]{0:T(1024)S(1)}, f32[1536]{0:T(1024)}, u32[]{:S(2)}) copy-start(f32[1536]{0:T(1024)} %copy-done.30) | copy-start | bytes 18436
  225.8 7.5 %copy-start.23 = (bf16[192,768]{1,0:T(8,128)(2,1)S(1)}, bf16[192,768]{1,0:T(8,128)(2,1)}, u32[]{:S(2)}) copy-start(bf16[192,768]{1,0:T(8,128)(2,1)} %param.28) | copy-start | bytes 884740
  253.3 9.5 %copy-start.6 = (f32[1536,3,64]{0,2,1:T(8,128)S(1)}, f32[1536,3,64]{0,2,1:T(8,128)}, u32[]{:S(2)}) copy-start(f32[1536,3,64]{0,2,1:T(8,128)} %get-tuple-element.453) | copy-start | bytes 3538948 | tf_op jit(solution)/shard_map/while
  266.3 7.7 %copy-start.7 = (f32[1536,3,64]{0,2,1:T(8,128)}, f32[1536,3,64]{0,2,1:T(8,128)S(1)}, u32[]{:S(2)}) copy-start(f32[1536,3,64]{0,2,1:T(8,128)S(1)} %fusion.123) | copy-start | bytes 3538948 | tf_op jit(solution)/shard_map/while
  274.0 7.2 %copy-start.58 = (s32[3]{0:T(128)}, s32[3]{0:T(128)S(1)}, u32[]{:S(2)}) copy-start(s32[3]{0:T(128)S(1)} %get-tuple-element.472) | copy-start | bytes 40 | tf_op jit(solution)/shard_map/while
  291.3 9.5 %copy-start.6 = (f32[1536,3,64]{0,2,1:T(8,128)S(1)}, f32[1536,3,64]{0,2,1:T(8,128)}, u32[]{:S(2)}) copy-start(f32[1536,3,64]{0,2,1:T(8,128)} %get-tuple-element.453) | copy-start | bytes 3538948 | tf_op jit(solution)/shard_map/while
  304.3 7.7 %copy-start.7 = (f32[1536,3,64]{0,2,1:T(8,128)}, f32[1536,3,64]{0,2,1:T(8,128)S(1)}, u32[]{:S(2)}) copy-start(f32[1536,3,64]{0,2,1:T(8,128)S(1)} %fusion.123) | copy-start | bytes 3538948 | tf_op jit(solution)/shard_map/while
  312.0 7.2 %copy-start.58 = (s32[3]{0:T(128)}, s32[3]{0:T(128)S(1)}, u32[]{:S(2)}) copy-start(s32[3]{0:T(128)S(1)} %get-tuple-element.472) | copy-start | bytes 40 | tf_op jit(solution)/shard_map/while
  329.4 9.5 %copy-start.6 = (f32[1536,3,64]{0,2,1:T(8,128)S(1)}, f32[1536,3,64]{0,2,1:T(8,128)}, u32[]{:S(2)}) copy-start(f32[1536,3,64]{0,2,1:T(8,128)} %get-tuple-element.453) | copy-start | bytes 3538948 | tf_op jit(solution)/shard_map/while
  342.4 7.7 %copy-start.7 = (f32[1536,3,64]{0,2,1:T(8,128)}, f32[1536,3,64]{0,2,1:T(8,128)S(1)}, u32[]{:S(2)}) copy-start(f32[1536,3,64]{0,2,1:T(8,128)S(1)} %fusion.123) | copy-start | bytes 3538948 | tf_op jit(solution)/shard_map/while
  358.8 239.0 %all-reduce.12.cloned.1.call-start = ((), (), s32[]{:S(2)}) async-start(), calls=%async_computation.2 | async-start | bytes 7077888 | tf_op jit(solution)/shard_map/psum | solution.py:180
  370.6 82.5 %copy-start.27 = (f32[1536]{0:T(1024)S(1)}, f32[1536]{0:T(1024)}, u32[]{:S(2)}) copy-start(f32[1536]{0:T(1024)} %copy-done.26) | copy-start | bytes 18436
  370.6 82.5 %copy-start.33 = (f32[768]{0:T(1024)S(1)}, f32[768]{0:T(1024)}, u32[]{:S(2)}) copy-start(f32[768]{0:T(1024)} %copy-done.32) | copy-start | bytes 9220
  372.1 85.8 %copy-start.37 = (f32[1536]{0:T(1024)S(1)}, f32[1536]{0:T(1024)}, u32[]{:S(2)}) copy-start(f32[1536]{0:T(1024)} %copy-done.36) | copy-start | bytes 18436
  372.1 85.8 %copy-start.29 = (f32[1536]{0:T(1024)S(1)}, f32[1536]{0:T(1024)}, u32[]{:S(2)}) copy-start(f32[1536]{0:T(1024)} %copy-done.28) | copy-start | bytes 18436
  457.9 49.7 %slice-start = ((s8[4718592]{0:T(1024)(128)(4,1)}), s8[524288]{0:T(1024)(128)(4,1)S(1)}, s32[]{:S(2)}) async-start(s8[4718592]{0:T(1024)(128)(4,1)} %bitcast.110), calls=%async_computation.4 | async-start | bytes 1048576
  597.8 8.1 %copy-start.1 = (bf16[768,768]{1,0:T(8,128)(2,1)S(1)}, bf16[768,768]{1,0:T(8,128)(2,1)}, u32[]{:S(2)}) copy-start(bf16[768,768]{1,0:T(8,128)(2,1)} %param.32) | copy-start | bytes 3538948
  597.8 7.2 %copy-start.25 = (bf16[192,768]{1,0:T(8,128)(2,1)S(1)}, bf16[192,768]{1,0:T(8,128)(2,1)}, u32[]{:S(2)}) copy-start(bf16[192,768]{1,0:T(8,128)(2,1)} %get-tuple-element.231) | copy-start | bytes 884740
  (58 other events, 197.9 us)
Sparse Core Ops, SparseCore 0:
  72.6 58.3 all-reduce.7
  159.5 55.7 all-reduce.9
  358.9 94.1 all-reduce.13
  458.0 139.6 all-reduce.11
where the time goes:
time: 620 us; the launch traced here: 613 us
  waiting for transfers between devices  269 us (43%)
  matrix products  139 us (22%)
  other arithmetic  116 us (19%)
  blocking collectives  40.5 us (7%)
  local copies, waits for them, and re-layouts  29.3 us (5%)
  between operations  15.1 us (2%)
    psum x1, waiting for transfers between devices, sum_gradients(): lax.psum([g.astype(jnp.bfloat16) for g, w in zip(grads, large) if w], 'dp')  84.2 us
    psum x1, waiting for transfers between devices, run_forward(): mlp_total = lax.psum(mlp_part, 'tensor').astype(jnp.float32)  80.8 us
    psum x1, waiting for transfers between devices, run_forward(): attn_total = lax.psum(attn_part, 'tensor').astype(jnp.float32)  53.4 us
    psum x1, waiting for transfers between devices, on_device(): lax.psum(norm_grad_part.astype(jnp.bfloat16), 'tensor').astype(jnp.float32)  50.4 us
    psum x1, blocking collectives, sum_gradients(): wide = lax.psum([g for g, w in zip(grads, large) if not w], 'dp')  40.5 us
    dot_general x6, matrix products, block_scores(): jnp.einsum('qhd,khd->hqk', query_block, key_rows, preferred_element_type=...  30.4 us
    convert_element_type x3, other arithmetic, back_block(): score_grad = (weights * (weight_grad - centre)).astype(jnp.bfloat16)  28.3 us
    reduce_sum x4, other arithmetic, layer_norm(): return centred * lax.rsqrt(spread + NORM_EPS) * norm_gain + norm_shift  19.6 us
  transfers between devices with their start and end apart: 4, of which 4 were waited for; matrix products, arithmetic and copies ran while one was open for 7% of the time, Pallas kernels for 0%

commit v1 on v0

--- a/solution.py
+++ b/solution.py
@@ -8,6 +8,10 @@
 HEAD_DIM = 64
 NORM_EPS = 1e-06
 MASK_FILL = -1e30
+
+
+def register_cubes(x_local):
+    return jnp.sum(jax.lax.all_gather(x_local, "tensor"), axis=0)
 
 
 def layer_norm(values_in, norm_gain, norm_shift):
@@ -146,7 +150,7 @@
     if second_pass:
         attn_total = lax.psum(attn_part, "tensor").astype(jnp.float32)
     else:
-        attn_total = lax.psum(attn_part, "tensor").astype(jnp.float32)
+        attn_total = register_cubes(attn_part).astype(jnp.float32)
     middle = hidden_in + attn_total + b_out.astype(jnp.float32)
     normed_two = layer_norm(
         middle, ln2_gain.astype(jnp.float32), ln2_shift.astype(jnp.float32)

time: 620 us -> 635 us (1.024)
  waiting for transfers between devices: 269 us -> 277 us
  other arithmetic: 116 us -> 123 us
    all_gather x0 -> x1, waiting for transfers between devices: none -> 62 us  [register_cubes(): return jnp.sum(jax.lax.all_gather(x_local, 'tensor'), axis=0)]
    psum x1 -> x0, waiting for transfers between devices: 53.4 us -> none  [run_forward(): attn_total = lax.psum(attn_part, 'tensor').astype(jnp.float32)]
    reduce_sum x0 -> x1, other arithmetic: none -> 7.13 us  [register_cubes(): return jnp.sum(jax.lax.all_gather(x_local, 'tensor'), axis=0)]
where the time goes in v1:
time: 635 us; the launch traced here: 628 us
  waiting for transfers between devices  277 us (44%)
  matrix products  139 us (22%)
  other arithmetic  123 us (19%)
  blocking collectives  40.6 us (6%)
  local copies, waits for them, and re-layouts  29.2 us (5%)
  between operations  14.8 us (2%)
    psum x1, waiting for transfers between devices, sum_gradients(): lax.psum([g.astype(jnp.bfloat16) for g, w in zip(grads, large) if w], 'dp')  84.1 us
    psum x1, waiting for transfers between devices, run_forward(): mlp_total = lax.psum(mlp_part, 'tensor').astype(jnp.float32)  80.8 us
    all_gather x1, waiting for transfers between devices, register_cubes(): return jnp.sum(jax.lax.all_gather(x_local, 'tensor'), axis=0)  62 us
    psum x1, waiting for transfers between devices, on_device(): lax.psum(norm_grad_part.astype(jnp.bfloat16), 'tensor').astype(jnp.float32)  50.3 us
    psum x1, blocking collectives, sum_gradients(): wide = lax.psum([g for g, w in zip(grads, large) if not w], 'dp')  40.6 us
    dot_general x6, matrix products, block_scores(): jnp.einsum('qhd,khd->hqk', query_block, key_rows, preferred_element_type=...  30.4 us
    convert_element_type x3, other arithmetic, back_block(): score_grad = (weights * (weight_grad - centre)).astype(jnp.bfloat16)  28.3 us
    reduce_sum x4, other arithmetic, layer_norm(): return centred * lax.rsqrt(spread + NORM_EPS) * norm_gain + norm_shift  19.9 us
  transfers between devices with their start and end apart: 4, of which 4 were waited for; matrix products, arithmetic and copies ran while one was open for 7% of the time, Pallas kernels for 0%

profile of v1, /device:TPU:0, one launch (start us, length us, event | category | flops | bytes accessed | tf_op | source)
XLA Modules:
  0.0 628.1 jit_solution(14172625536550729564)
XLA Ops:
  8.1 8.3 %multiply_sine_fusion = (f32[3,1536,128]{2,1,0:T(8,128)S(1)}, f32[3,1536,128]{2,1,0:T(8,128)S(1)}) fusion(f32[128]{0:T(128)S(1)} %negate_power_fusion, f32[3,1536]{1,0:T(4,128)S(1)} %convert_element_type.155), kind=kLoop, calls=%fused_computation.89 | loop fusion | flops 589824 | bytes 4737536 | tf_op jit(solution)/shard_map/sin | solution.py:29
  29.3 38.7 %while.27 = (s32[]{:T(128)}, bf16[3,512,3,64]{1,3,2,0:T(8,128)(2,1)S(1)}, f32[3,3,512]{2,1,0:T(4,128)}, s32[3]{0:T(128)S(1)}, s32[1536]{0:T(1024)}, /*index=5*/s...) while((s32[]{:T(128)}, ...), condition=%wide.region_7.8_spmd, body=%wide.region_4.7_spmd.sunk | while | flops 633076224 | bytes 33307488 | solution.py:68
  77.2 62.0 %all-gather.3.cloned.1.call-done = bf16[6144,768]{1,0:T(8,128)(2,1)} async-done(((bf16[1536,768]{1,0:T(8,128)(2,1)}), bf16[6144,768]{1,0:T(8,128)(2,1)}) %all-gather.3.cloned.1.call-update) | async-done | bytes 9437200 | tf_op jit(solution)/shard_map/all_gather | solution.py:14
  139.2 7.1 %reduce_sum.192 = bf16[1536,768]{1,0:T(8,128)(2,1)} reduce(bf16[4,1536,768]{2,1,0:T(8,128)(2,1)} %bitcast.116, bf16[]{:T(256)} %constant.32.clone.1), dimensions={0}, to_apply=%region_8.9 | reduce | flops 3538944 | bytes 11796482 | tf_op jit(solution)/shard_map/reduce_sum | solution.py:14
  152.4 12.8 %multiply_convert_fusion.1 = (bf16[1536,768]{1,0:T(8,128)(2,1)}, f32[1536,768]{1,0:T(8,128)S(1)}, f32[1536,768]{1,0:T(8,128)S(1)}) fusion(f32[768]{0:T(1024)S(1)} %copy-done.49, bf16[1536,768]{1,0:T(8,128)(2,1)S(1)} %add_convert_fusion.1, bf16[768,768]{1,0:T(8,128)(2,1)S(1)} %copy-done), kind=kOutput, calls=%fused_computation.69 | convolution fusion | flops 1889796096 | bytes 15338496 | tf_op jit(solution)/shard_map/dot_general | solution.py:158
  165.2 4.6 convert_reduce_fusion.3
  174.8 5.4 convolution_convert_fusion.1
  180.2 50.3 %all-reduce.7.cloned.1.call-done = bf16[1536,768]{1,0:T(8,128)(2,1)} async-done(((bf16[1536,768]{1,0:T(8,128)(2,1)}), bf16[1536,768]{1,0:T(8,128)(2,1)}) %all-reduce.7.cloned.1.call-update) | async-done | bytes 2359312 | tf_op jit(solution)/shard_map/psum | solution.py:250
  230.5 5.3 convert_reduce_fusion.1
  235.9 5.5 fusion.38
  241.4 5.2 fusion.57
  251.5 114.2 %while.28 = (s32[]{:T(128)}, f32[1536,3,64]{0,2,1:T(8,128)}, f32[1536,3,64]{0,2,1:T(8,128)S(1)}, bf16[3,512,3,64]{1,3,2,0:T(8,128)(2,1)}, s32[3]{0:T(128)S(1)}, ...) while((s32[]{:T(128)}, f32[1536,3,64]{0,2,1:T(8,128)}, ...), condition=%wide.region_17.18_spmd.clone, body=%wide.region_15.17_spmd.clone.sunk | while | flops 1533540864 | bytes 113105432 | solution.py:112
  252.6 6.0 fusion.122
  260.6 8.1 %multiply_reduce_fusion.4 = (f32[3,512]{1,0:T(4,128)S(1)}, f32[3,512,1536]{2,1,0:T(8,128)}) fusion(f32[3,512,1536]{2,1,0:T(8,128)} %fusion.122, f32[3,512]{1,0:T(4,128)S(1)} %dynamic-slice_bitcast_fusion.2, bf16[1536,3,64]{0,2,1:T(8,128)(2,1)S(1)} %get-tuple-element.476, bf16[1536,3,64]{0,2,1:T(8,128)(2,1)} %get-tuple-element.473, ...), kind=kOutput, calls=%fused_computation.16.clone.1 | convolution fusion | flops 313784832 | bytes 20459524 | tf_op jit(solution)/shard_map/while/body/eval_jaxpr/qhd,khd->hqk/dot_general | solution.py:45
  268.8 9.4 %multiply_convert_fusion.3 = bf16[3,512,1536]{2,1,0:T(8,128)(2,1)} fusion(f32[3,512,1536]{2,1,0:T(8,128)} %get-tuple-element.395, f32[3,512,1536]{2,1,0:T(8,128)} %fusion.122, f32[3,512]{1,0:T(4,128)S(1)} %get-tuple-element.396), kind=kLoop, calls=%fused_computation.15.clone.1 | loop fusion | flops 7077888 | bytes 23599104 | tf_op jit(solution)/shard_map/while/body/eval_jaxpr/convert_element_type | solution.py:91
  284.6 4.9 fusion.124
  290.7 6.0 fusion.122
  298.7 8.1 %multiply_reduce_fusion.4 = (f32[3,512]{1,0:T(4,128)S(1)}, f32[3,512,1536]{2,1,0:T(8,128)}) fusion(f32[3,512,1536]{2,1,0:T(8,128)} %fusion.122, f32[3,512]{1,0:T(4,128)S(1)} %dynamic-slice_bitcast_fusion.2, bf16[1536,3,64]{0,2,1:T(8,128)(2,1)S(1)} %get-tuple-element.476, bf16[1536,3,64]{0,2,1:T(8,128)(2,1)} %get-tuple-element.473, ...), kind=kOutput, calls=%fused_computation.16.clone.1 | convolution fusion | flops 313784832 | bytes 20459524 | tf_op jit(solution)/shard_map/while/body/eval_jaxpr/qhd,khd->hqk/dot_general | solution.py:45
  306.9 9.4 %multiply_convert_fusion.3 = bf16[3,512,1536]{2,1,0:T(8,128)(2,1)} fusion(f32[3,512,1536]{2,1,0:T(8,128)} %get-tuple-element.395, f32[3,512,1536]{2,1,0:T(8,128)} %fusion.122, f32[3,512]{1,0:T(4,128)S(1)} %get-tuple-element.396), kind=kLoop, calls=%fused_computation.15.clone.1 | loop fusion | flops 7077888 | bytes 23599104 | tf_op jit(solution)/shard_map/while/body/eval_jaxpr/convert_element_type | solution.py:91
  322.7 4.9 fusion.124
  328.8 6.0 fusion.122
  336.8 8.1 %multiply_reduce_fusion.4 = (f32[3,512]{1,0:T(4,128)S(1)}, f32[3,512,1536]{2,1,0:T(8,128)}) fusion(f32[3,512,1536]{2,1,0:T(8,128)} %fusion.122, f32[3,512]{1,0:T(4,128)S(1)} %dynamic-slice_bitcast_fusion.2, bf16[1536,3,64]{0,2,1:T(8,128)(2,1)S(1)} %get-tuple-element.476, bf16[1536,3,64]{0,2,1:T(8,128)(2,1)} %get-tuple-element.473, ...), kind=kOutput, calls=%fused_computation.16.clone.1 | convolution fusion | flops 313784832 | bytes 20459524 | tf_op jit(solution)/shard_map/while/body/eval_jaxpr/qhd,khd->hqk/dot_general | solution.py:45
  344.9 9.4 %multiply_convert_fusion.3 = bf16[3,512,1536]{2,1,0:T(8,128)(2,1)} fusion(f32[3,512,1536]{2,1,0:T(8,128)} %get-tuple-element.395, f32[3,512,1536]{2,1,0:T(8,128)} %fusion.122, f32[3,512]{1,0:T(4,128)S(1)} %get-tuple-element.396), kind=kLoop, calls=%fused_computation.15.clone.1 | loop fusion | flops 7077888 | bytes 23599104 | tf_op jit(solution)/shard_map/while/body/eval_jaxpr/convert_element_type | solution.py:91
  360.7 4.9 fusion.124
  369.6 4.6 bitcast_convert_fusion
  374.4 5.6 convolution_convert_fusion.5
  387.8 80.8 %all-reduce.11.cloned.1.call-done = (bf16[1536,768]{1,0:T(8,128)(2,1)}, bf16[1536,768]{1,0:T(8,128)(2,1)}) async-done(((bf16[1536,768]{1,0:T(8,128)(2,1)}, bf16[1536,768]{1,0:T(8,128)(2,1)}), (bf16[1536,768]{1,0:T(8,128)(2,1)}, bf16[1536,768]{1,0:T(8,128)(2,1)})) %all-reduce.11.cloned.1.call-update) | async-done | bytes 4718608 | tf_op jit(solution)/shard_map/psum | solution.py:177
  468.6 4.7 convert_reduce_fusion
  477.8 40.6 %all-reduce = (f32[768]{0:T(1024)}, f32[768]{0:T(1024)}, f32[2,192]{1,0:T(2,128)}, f32[768]{0:T(1024)}, f32[768]{0:T(1024)}, /*index=5*/f32[768]{0:T(1024)}, f32[768]{0:T(1024)}, f32[768]{0:T(1024)}) all-reduce(f32[768]{0:T(1024)S(1)} %get-tuple-element.172, ...), channel_id=1, replica_groups=mesh['dp'=8,'tensor'=4] {'dp'}, use_global_device_ids=true, to_apply=%region_22.23 | all-reduce | flops 5760 | bytes 46080 | tf_op jit(solution)/shard_map/psum | solution.py:185
  518.5 4.8 select_convert_fusion
  524.4 4.8 add_add_fusion.2
  529.2 84.1 %all-reduce.9.cloned.1.call-done = (bf16[768,3,192]{0,2,1:T(8,128)(2,1)}, bf16[192,768]{1,0:T(8,128)(2,1)}, bf16[768,768]{1,0:T(8,128)(2,1)}, bf16[768,768]{1,0:T(8,128)(2,1)}) async-done(((bf16[768,3,192]{0,2,1:T(8,128)(2,1)}, bf16[192,768]{1,0:T(8,128)(2,1)}, bf16[768,768]{1,0:T(8,128)(2,1)}, bf16[768,768]{1,0:T(8,128)(2,1)}), (bf16[768,3,192]{0,2,1:T(8,128)(2,1)}, bf16[192,768]{1,0:T(8,128)(2,1)}, ...) | async-done | bytes 3538960 | tf_op jit(solution)/shard_map/psum | solution.py:184
  (291 shorter events, 126.9 us)
Async XLA Ops:
  7.2 145.2 %copy-start = (bf16[768,768]{1,0:T(8,128)(2,1)S(1)}, bf16[768,768]{1,0:T(8,128)(2,1)}, u32[]{:S(2)}) copy-start(bf16[768,768]{1,0:T(8,128)(2,1)} %param.32) | copy-start | bytes 3538948
  7.2 132.0 %all-gather.3.cloned.1.call-start = ((), (), s32[]{:S(2)}) async-start(), calls=%async_computation.1 | async-start | bytes 11796480 | tf_op jit(solution)/shard_map/all_gather | solution.py:14
  68.0 78.4 %copy-start.8 = (bf16[1536,3,64]{0,2,1:T(8,128)(2,1)}, bf16[1536,3,64]{0,2,1:T(8,128)(2,1)S(1)}, u32[]{:S(2)}) copy-start(bf16[1536,3,64]{0,2,1:T(8,128)(2,1)S(1)} %get-tuple-element.500) | copy-start | bytes 1769476
  68.7 77.7 %copy-start.12 = (bf16[24,8,3,512]{3,1,2,0:T(8,128)(2,1)}, bf16[24,8,3,512]{3,1,2,0:T(8,128)(2,1)S(1)}, u32[]{:S(2)}) copy-start(bf16[24,8,3,512]{3,1,2,0:T(8,128)(2,1)S(1)} %copy.35) | copy-start | bytes 1769476
  72.1 158.4 %all-reduce.7.cloned.1.call-start = ((), (), s32[]{:S(2)}) async-start(), calls=%async_computation | async-start | bytes 4718592 | tf_op jit(solution)/shard_map/psum | solution.py:250
  150.9 14.3 %copy-start.38 = (f32[1536]{0:T(1024)}, f32[1536]{0:T(1024)S(1)}, u32[]{:S(2)}) copy-start(f32[1536]{0:T(1024)S(1)} %multiply_reduce_fusion.1) | copy-start | bytes 18436
  150.9 14.3 %copy-start.30 = (f32[1536]{0:T(1024)}, f32[1536]{0:T(1024)S(1)}, u32[]{:S(2)}) copy-start(f32[1536]{0:T(1024)S(1)} %fusion.53) | copy-start | bytes 18436
  152.4 12.8 %copy-start.22 = (bf16[1536,768]{1,0:T(8,128)(2,1)}, bf16[1536,768]{1,0:T(8,128)(2,1)S(1)}, u32[]{:S(2)}) copy-start(bf16[1536,768]{1,0:T(8,128)(2,1)S(1)} %add_convert_fusion.1) | copy-start | bytes 7077892
  152.4 12.8 %copy-start.17 = (bf16[1536,768]{1,0:T(8,128)(2,1)S(1)}, bf16[1536,768]{1,0:T(8,128)(2,1)}, u32[]{:S(2)}) copy-start(bf16[1536,768]{1,0:T(8,128)(2,1)} %param.23) | copy-start | bytes 7077892
  152.4 12.8 %copy-start.40 = (pred[1536]{0:T(1024)(128)(4,1)S(1)}, pred[1536]{0:T(1024)(128)(4,1)}, u32[]{:S(2)}) copy-start(pred[1536]{0:T(1024)(128)(4,1)} %iota_compare_fusion.1) | copy-start | bytes 4612
  152.4 12.8 %copy-start.55 = (bf16[768,768]{1,0:T(8,128)(2,1)S(1)}, bf16[768,768]{1,0:T(8,128)(2,1)}, u32[]{:S(2)}) copy-start(bf16[768,768]{1,0:T(8,128)(2,1)} %param.34) | copy-start | bytes 3538948
  174.7 293.9 %all-reduce.11.cloned.1.call-start = ((), (), s32[]{:S(2)}) async-start(), calls=%async_computation.3 | async-start | bytes 9437184 | tf_op jit(solution)/shard_map/psum | solution.py:177
  174.8 55.7 %copy-start.35 = (f32[768]{0:T(1024)S(1)}, f32[768]{0:T(1024)}, u32[]{:S(2)}) copy-start(f32[768]{0:T(1024)} %convert_element_type.168) | copy-start | bytes 9220
  180.2 55.7 %copy-start.39 = (f32[1536]{0:T(1024)S(1)}, f32[1536]{0:T(1024)}, u32[]{:S(2)}) copy-start(f32[1536]{0:T(1024)} %copy-done.38) | copy-start | bytes 18436
  180.2 55.7 %copy-start.31 = (f32[1536]{0:T(1024)S(1)}, f32[1536]{0:T(1024)}, u32[]{:S(2)}) copy-start(f32[1536]{0:T(1024)} %copy-done.30) | copy-start | bytes 18436
  241.4 7.5 %copy-start.23 = (bf16[192,768]{1,0:T(8,128)(2,1)S(1)}, bf16[192,768]{1,0:T(8,128)(2,1)}, u32[]{:S(2)}) copy-start(bf16[192,768]{1,0:T(8,128)(2,1)} %param.28) | copy-start | bytes 884740
  268.8 9.5 %copy-start.6 = (f32[1536,3,64]{0,2,1:T(8,128)S(1)}, f32[1536,3,64]{0,2,1:T(8,128)}, u32[]{:S(2)}) copy-start(f32[1536,3,64]{0,2,1:T(8,128)} %get-tuple-element.453) | copy-start | bytes 3538948 | tf_op jit(solution)/shard_map/while
  281.8 7.7 %copy-start.7 = (f32[1536,3,64]{0,2,1:T(8,128)}, f32[1536,3,64]{0,2,1:T(8,128)S(1)}, u32[]{:S(2)}) copy-start(f32[1536,3,64]{0,2,1:T(8,128)S(1)} %fusion.123) | copy-start | bytes 3538948 | tf_op jit(solution)/shard_map/while
  289.5 7.2 %copy-start.58 = (s32[3]{0:T(128)}, s32[3]{0:T(128)S(1)}, u32[]{:S(2)}) copy-start(s32[3]{0:T(128)S(1)} %get-tuple-element.472) | copy-start | bytes 40 | tf_op jit(solution)/shard_map/while
  306.9 9.5 %copy-start.6 = (f32[1536,3,64]{0,2,1:T(8,128)S(1)}, f32[1536,3,64]{0,2,1:T(8,128)}, u32[]{:S(2)}) copy-start(f32[1536,3,64]{0,2,1:T(8,128)} %get-tuple-element.453) | copy-start | bytes 3538948 | tf_op jit(solution)/shard_map/while
  319.9 7.7 %copy-start.7 = (f32[1536,3,64]{0,2,1:T(8,128)}, f32[1536,3,64]{0,2,1:T(8,128)S(1)}, u32[]{:S(2)}) copy-start(f32[1536,3,64]{0,2,1:T(8,128)S(1)} %fusion.123) | copy-start | bytes 3538948 | tf_op jit(solution)/shard_map/while
  327.6 7.2 %copy-start.58 = (s32[3]{0:T(128)}, s32[3]{0:T(128)S(1)}, u32[]{:S(2)}) copy-start(s32[3]{0:T(128)S(1)} %get-tuple-element.472) | copy-start | bytes 40 | tf_op jit(solution)/shard_map/while
  344.9 9.5 %copy-start.6 = (f32[1536,3,64]{0,2,1:T(8,128)S(1)}, f32[1536,3,64]{0,2,1:T(8,128)}, u32[]{:S(2)}) copy-start(f32[1536,3,64]{0,2,1:T(8,128)} %get-tuple-element.453) | copy-start | bytes 3538948 | tf_op jit(solution)/shard_map/while
  358.0 7.7 %copy-start.7 = (f32[1536,3,64]{0,2,1:T(8,128)}, f32[1536,3,64]{0,2,1:T(8,128)S(1)}, u32[]{:S(2)}) copy-start(f32[1536,3,64]{0,2,1:T(8,128)S(1)} %fusion.123) | copy-start | bytes 3538948 | tf_op jit(solution)/shard_map/while
  374.3 239.0 %all-reduce.9.cloned.1.call-start = ((), (), s32[]{:S(2)}) async-start(), calls=%async_computation.2 | async-start | bytes 7077888 | tf_op jit(solution)/shard_map/psum | solution.py:184
  386.1 82.5 %copy-start.27 = (f32[1536]{0:T(1024)S(1)}, f32[1536]{0:T(1024)}, u32[]{:S(2)}) copy-start(f32[1536]{0:T(1024)} %copy-done.26) | copy-start | bytes 18436
  386.1 82.5 %copy-start.33 = (f32[768]{0:T(1024)S(1)}, f32[768]{0:T(1024)}, u32[]{:S(2)}) copy-start(f32[768]{0:T(1024)} %copy-done.32) | copy-start | bytes 9220
  387.6 85.8 %copy-start.37 = (f32[1536]{0:T(1024)S(1)}, f32[1536]{0:T(1024)}, u32[]{:S(2)}) copy-start(f32[1536]{0:T(1024)} %copy-done.36) | copy-start | bytes 18436
  387.6 85.8 %copy-start.29 = (f32[1536]{0:T(1024)S(1)}, f32[1536]{0:T(1024)}, u32[]{:S(2)}) copy-start(f32[1536]{0:T(1024)} %copy-done.28) | copy-start | bytes 18436
  473.4 49.8 %slice-start = ((s8[4718592]{0:T(1024)(128)(4,1)}), s8[524288]{0:T(1024)(128)(4,1)S(1)}, s32[]{:S(2)}) async-start(s8[4718592]{0:T(1024)(128)(4,1)} %bitcast.111), calls=%async_computation.4 | async-start | bytes 1048576
  613.3 8.1 %copy-start.1 = (bf16[768,768]{1,0:T(8,128)(2,1)S(1)}, bf16[768,768]{1,0:T(8,128)(2,1)}, u32[]{:S(2)}) copy-start(bf16[768,768]{1,0:T(8,128)(2,1)} %param.32) | copy-start | bytes 3538948
  613.3 7.2 %copy-start.25 = (bf16[192,768]{1,0:T(8,128)(2,1)S(1)}, bf16[192,768]{1,0:T(8,128)(2,1)}, u32[]{:S(2)}) copy-start(bf16[192,768]{1,0:T(8,128)(2,1)} %get-tuple-element.231) | copy-start | bytes 884740
  (58 other events, 198.5 us)
Sparse Core Ops, SparseCore 0:
  72.2 66.9 all-gather.2
  174.8 55.6 all-reduce.6
  374.4 94.1 all-reduce.10
  473.5 139.6 all-reduce.8
